TPU v7x, 32 devices: a whole 2x2x4 slice. The times are simulated.
32 devices in a mesh: seg: 4 (over y, core), tm: 8 (over z, x).
Axes of the slice: x: 2, y: 2, z: 4, core: 2. Of those that a mesh axis runs over, the one named last changes fastest.
Arguments:
- transition: bfloat16 [64, 512, 512], P(('seg', 'tm')), may hold values from -1 to 1
- obs_gain: bfloat16 [64, 512, 512], P(('seg', 'tm')), may hold values from -0.0625 to 0.0625
- observed: bfloat16 [64, 4, 512], P(('seg', 'tm')), may hold values from -6 to 6
- init_mean: float32 [4, 512], replicated, may hold values from -6 to 6
- init_factor: float32 [512, 512], P('tm'), may hold values from -6 to 6
Outputs:
- means: float32 [64, 4, 512], P(('seg', 'tm'))
- factor_ends: float32 [4, 512, 512], P('seg', 'tm')
All inputs are finite; a program needn't handle non-finite values.
Results may differ from a plain program's by a relative error of at most 0.0003.
Values sent between devices are 32-bit elements; how exact they have to be, the bound alone decides.
No kernel may reach another device: no remote copies, remote signals or barrier semaphores. Data moves between devices by JAX's collectives and lax.ppermute only.
A program may use at most 128 MiB of HBM per device.

v0:
```python
import jax
import jax.numpy as jnp
from jax import lax
from jax.experimental import pallas as pl
from jax.experimental.pallas import tpu as pltpu
from jax.sharding import PartitionSpec as P

F32 = jnp.float32
BF16 = jnp.bfloat16
AXES = ("seg", "tm")
GRANT = 10 * 1024 * 1024
AHEAD = 2


def halves(x):
    hi = x.astype(BF16)
    return hi, (x - hi.astype(F32)).astype(BF16)


def dot(a, b):
    return jnp.dot(a, b, preferred_element_type=F32)


def dot3(a_hi, a_lo, b_hi, b_lo):
    return dot(a_hi, b_hi) + (dot(a_hi, b_lo) + dot(a_lo, b_hi))


def few(rows, hi, lo=None):
    r_hi = rows.astype(BF16)
    r_hi32 = r_hi.astype(F32)
    both = jnp.concatenate([r_hi32, rows - r_hi32]).astype(BF16)
    res = dot(both, hi)
    res = res[: rows.shape[0]] + res[rows.shape[0] :]
    return res if lo is None else res + dot(r_hi, lo)


class Sizes:
    def __init__(self, width, series, chunks):
        self.width, self.series, self.chunks = width, series, chunks
        self.part = width // chunks
        self.tall = width + 16 * (-(-series // 16))
        self.buf = width + 8 * (-(-chunks * series // 8))
        self.low = self.tall - width


def put_rows(z, out, body, tail):
    for j in range(z.chunks):
        cols = slice(j * z.part, (j + 1) * z.part)
        out[j * z.part : (j + 1) * z.part, :] = body[:, cols]
        out[z.width + j * z.series : z.width + (j + 1) * z.series, :] = tail[:, cols]


def put_cols(z, out, body, tail):
    out[: z.width, :] = body
    out[z.width : z.width + z.series, :] = tail


def gather_rows(z, bufs, full):
    for k, buf in enumerate(bufs):
        for j in range(z.chunks):
            full[k * z.part : (k + 1) * z.part, j * z.part : (j + 1) * z.part] = buf[j * z.part : (j + 1) * z.part, :]
    for j in range(z.chunks):
        full[z.width : z.width + z.series, j * z.part : (j + 1) * z.part] = bufs[0][
            z.width + j * z.series : z.width + (j + 1) * z.series, :
        ]


def gather_cols(z, bufs, full):
    for k, buf in enumerate(bufs):
        cols = slice(k * z.part, (k + 1) * z.part)
        full[: z.width, cols] = buf[: z.width, :]
        full[z.width : z.width + z.series, cols] = buf[z.width : z.width + z.series, :]


def clear_low(z, full):
    full[z.width :, :] = jnp.zeros((z.low, z.width), F32)


def put_chunks(z, by_rows, outs, full):
    @pl.when(by_rows)
    def _():
        for k, out in enumerate(outs):
            put_rows(z, out, full[k * z.part : (k + 1) * z.part, :], full[z.width : z.width + z.series, :])

    @pl.when(jnp.logical_not(by_rows))
    def _():
        for k, out in enumerate(outs):
            cols = slice(k * z.part, (k + 1) * z.part)
            put_cols(z, out, full[: z.width, cols], full[z.width : z.width + z.series, cols])


def call(kernel, outs, operands, where=None, scratch=(), far=0):
    in_specs = [pl.BlockSpec(memory_space=pltpu.HBM if i < far else pltpu.VMEM) for i in range(len(operands))]
    operands = [pltpu.with_memory_space_constraint(x, pltpu.HBM) if i < far else x for i, x in enumerate(operands)]

    def body(*refs):
        if where is None:
            kernel(*refs)
        else:
            kernel(where(lax.axis_index("seg"), lax.axis_index("tm")), *refs)

    return pl.pallas_call(
        body,
        out_shape=outs,
        in_specs=in_specs,
        out_specs=jax.tree.map(lambda _: pl.BlockSpec(memory_space=pltpu.VMEM), outs),
        scratch_shapes=list(scratch),
        compiler_params=pltpu.CompilerParams(vmem_limit_bytes=GRANT),
    )(*operands)


def shape(rows, cols, dtype=F32):
    return jax.ShapeDtypeStruct((rows, cols), dtype)


def gather(z, by_rows, bufs, full):
    @pl.when(by_rows)
    def _():
        gather_rows(z, bufs, full)

    @pl.when(jnp.logical_not(by_rows))
    def _():
        gather_cols(z, bufs, full)


def map_shapes(z):
    return [shape(z.tall, z.width, BF16), shape(z.tall, z.width, BF16), shape(z.series, z.width)]


def local_map(z, where, transition, gain, observed):
    steps = transition.shape[0]

    def kernel(by_rows, t_hbm, g_hbm, o_hbm, *rest):
        chunks, (whole, hi, lo, tail, drive) = rest[: z.chunks], rest[z.chunks : z.chunks + 5]
        t, g, o, sems = rest[z.chunks + 5 :]
        copies = [
            pltpu.make_async_copy(t_hbm, t, sems.at[0]),
            pltpu.make_async_copy(g_hbm, g, sems.at[1]),
            pltpu.make_async_copy(o_hbm, o, sems.at[2]),
        ]
        for copy in copies:
            copy.start()
        copies[0].wait()
        body = t[0]
        for i in range(1, steps):
            if i == 1:
                body = dot(body, t[i])
            else:
                b_hi, b_lo = halves(body)
                body = dot(b_hi, t[i]) + dot(b_lo, t[i])
        clear_low(z, whole)
        whole[: z.width, :] = body.astype(F32)
        copies[1].wait()
        copies[2].wait()
        drives = [dot(o[i], g[i]) for i in range(steps)]
        low = drives[0]
        for i in range(steps):
            drive[i] = drives[i]
            if i:
                l_hi, l_lo = halves(low)
                low = dot(l_hi, t[i]) + dot(l_lo, t[i]) + drives[i]
        whole[z.width : z.width + z.series, :] = low
        tail[...] = low
        put_chunks(z, by_rows, chunks, whole)
        hi[...], lo[...] = halves(whole[...])

    res = call(
        kernel,
        [shape(z.buf, z.part)] * z.chunks
        + [shape(z.tall, z.width)]
        + map_shapes(z)
        + [jax.ShapeDtypeStruct((steps, z.series, z.width), F32)],
        [transition, gain, observed],
        where,
        scratch=[
            pltpu.VMEM(transition.shape, transition.dtype),
            pltpu.VMEM(gain.shape, gain.dtype),
            pltpu.VMEM(observed.shape, observed.dtype),
            pltpu.SemaphoreType.DMA((3,)),
        ],
        far=3,
    )
    n = z.chunks
    return res[:n], res[n], tuple(res[n + 1 : n + 4]), res[n + 4]


def times_chunk(z, where, chunk, own):
    def kernel(by_rows, got, own_hi, own_lo, own_tail, out, left):
        @pl.when(by_rows)
        def _():
            left[z.part :, :] = jnp.zeros((left.shape[0] - z.part, z.width), F32)
            for j in range(z.chunks):
                cols = slice(j * z.part, (j + 1) * z.part)
                left[: z.part, cols] = got[j * z.part : (j + 1) * z.part, :]
                left[z.part : z.part + z.series, cols] = got[z.width + j * z.series : z.width + (j + 1) * z.series, :]
            l_hi, l_lo = halves(left[...])
            res = dot3(l_hi, l_lo, own_hi[: z.width, :], own_lo[: z.width, :])
            put_rows(z, out, res[: z.part], res[z.part : z.part + z.series] + own_tail[...])

        @pl.when(jnp.logical_not(by_rows))
        def _():
            r_hi, r_lo = halves(got[: z.width, :])
            res = dot3(own_hi[...], own_lo[...], r_hi, r_lo)
            out[z.width :, :] = jnp.zeros((z.buf - z.width, z.part), F32)
            put_cols(z, out, res[: z.width], res[z.width : z.width + z.series] + got[z.width : z.width + z.series, :])

    return call(
        kernel, shape(z.buf, z.part), [chunk, *own], where, scratch=[pltpu.VMEM((z.part + z.low, z.width), F32)]
    )


def merge(z, where, got, own):
    def kernel(flag, *refs):
        by_rows, got_left, next_rows = flag
        n = z.chunks
        gots, owns = refs[:n], refs[n : 2 * n]
        outs = refs[2 * n : 3 * n]
        hi, lo, tail, left_hi, left_lo, left_tail = refs[3 * n : 3 * n + 6]
        a, b, c = refs[3 * n + 6 :]
        clear_low(z, a)
        clear_low(z, b)

        @pl.when(got_left)
        def _():
            gather(z, by_rows, gots, a)
            gather(z, by_rows, owns, b)

        @pl.when(jnp.logical_not(got_left))
        def _():
            gather(z, by_rows, owns, a)
            gather(z, by_rows, gots, b)

        left_hi[...], left_lo[...] = halves(a[...])
        left_tail[...] = a[z.width : z.width + z.series, :]
        r_hi, r_lo = halves(b[: z.width, :])
        c[...] = dot3(left_hi[...], left_lo[...], r_hi, r_lo)
        c[z.width : z.width + z.series, :] = c[z.width : z.width + z.series, :] + b[z.width : z.width + z.series, :]
        put_chunks(z, next_rows, outs, c)
        hi[...], lo[...] = halves(c[...])
        tail[...] = c[z.width : z.width + z.series, :]

    res = call(
        kernel,
        [shape(z.buf, z.part)] * z.chunks + map_shapes(z) * 2,
        list(got) + list(own),
        where,
        scratch=[pltpu.VMEM((z.tall, z.width), F32)] * 3,
    )
    n = z.chunks
    return res[:n], tuple(res[n : n + 3]), tuple(res[n + 3 :])


def assemble(z, where, chunks, others=None):
    extra = [] if others is None else list(others)

    def kernel(flag, *refs):
        by_rows, swap = flag
        n = z.chunks
        bufs, rest = refs[:n], refs[n : n + len(extra)]
        hi, lo, tail, full = refs[n + len(extra) :]
        clear_low(z, full)
        if not extra:
            gather(z, by_rows, bufs, full)
        else:

            @pl.when(jnp.logical_not(swap))
            def _():
                gather(z, by_rows, bufs, full)

            @pl.when(swap)
            def _():
                if len(rest) == 1:
                    full[...] = rest[0][...]
                else:
                    gather(z, by_rows, rest, full)

        hi[...], lo[...] = halves(full[...])
        tail[...] = full[z.width : z.width + z.series, :]

    return call(kernel, map_shapes(z), list(chunks) + extra, where, scratch=[pltpu.VMEM((z.tall, z.width), F32)])


def padded(series):
    return 8 * (-(-series // 8))


def advance(z, where, parts, block, before=None, split=False):
    low = padded(z.series)
    joined = len(parts) == 1
    rows = parts[0].shape[0] - low if joined else sum(p.shape[0] for p in parts[:-1])
    operands = list(parts) + list(block) + ([] if before is None else [before])

    def kernel(active, *refs):
        given, (hi, lo, tail) = refs[: len(parts)], refs[len(parts) : len(parts) + 3]
        outs, now = refs[len(operands) : -1], refs[-1]

        def put(value):
            if split:
                outs[0][...] = value[: rows // 2]
                outs[1][...] = value[rows // 2 : rows]
            else:
                outs[0][...] = value

        def run():
            if joined:
                state = given[0][...]
            else:
                now[rows:, :] = jnp.zeros((low, z.width), F32)
                at = 0
                for part in given:
                    now[at : at + part.shape[0], :] = part[...]
                    at += part.shape[0]
                state = now[...]
            now[...] = few(state, hi[: z.width, :], lo[: z.width, :])
            now[rows : rows + z.series, :] = now[rows : rows + z.series, :] + tail[...]
            put(now[...])

        if before is None:
            run()
        else:
            pl.when(active)(run)

            @pl.when(jnp.logical_not(active))
            def _():
                put(refs[len(operands) - 1][...])

    outs = [shape(rows // 2, z.width)] * 2 if split else [shape(rows + low, z.width)]
    res = call(kernel, outs, operands, where, scratch=[pltpu.VMEM((rows + low, z.width), F32)])
    return res if split else res[0]


def deal(where, kept, got):
    def kernel(received, a, b, out):
        @pl.when(received)
        def _():
            out[0] = b[...]

        @pl.when(jnp.logical_not(received))
        def _():
            out[0] = a[...]

    return call(kernel, jax.ShapeDtypeStruct((1, *kept.shape), F32), [kept, got], where)


def load_choice(z, index, refs, into):
    for i, ref in enumerate(refs):

        @pl.when(index == i)
        def _():
            if ref.shape[0] == z.series:
                into[...] = jnp.zeros(into.shape, F32)
                into[: z.series, :] = ref[...]
            else:
                into[...] = ref[ref.shape[0] - into.shape[0] :, :]


def descend(z, where, candidates, left, cross=None):
    low = padded(z.series)
    m = len(candidates)
    maps = list(left) + ([] if cross is None else list(cross))

    def kernel(flag, *refs):
        index, through, in_right = flag
        hi, lo, tail = refs[m : m + 3]
        mine, other, now = refs[m + len(maps) :]
        load_choice(z, index, refs[:m], now)
        if cross is not None:

            @pl.when(through)
            def _():
                c_hi, c_lo, c_tail = refs[m + 3 : m + 6]
                now[...] = few(now[...], c_hi[: z.width, :], c_lo[: z.width, :])
                now[: z.series, :] = now[: z.series, :] + c_tail[...]

        beyond = few(now[...], hi[: z.width, :], lo[: z.width, :])

        @pl.when(in_right)
        def _():
            mine[...] = beyond
            mine[: z.series, :] = mine[: z.series, :] + tail[...]
            other[...] = now[...]

        @pl.when(jnp.logical_not(in_right))
        def _():
            other[...] = beyond
            other[: z.series, :] = other[: z.series, :] + tail[...]
            mine[...] = now[...]

    return call(
        kernel, [shape(low, z.width)] * 2, [*candidates, *maps], where, scratch=[pltpu.VMEM((low, z.width), F32)]
    )


def last_steps(z, where, candidates, left, transition, drive):
    steps = transition.shape[0]
    m = len(candidates)
    low = padded(z.series)

    def kernel(flag, *refs):
        index, through = flag
        hi, lo, tail, t, d, out, now = refs[m:]
        load_choice(z, index, refs[:m], now)

        @pl.when(through)
        def _():
            now[...] = few(now[...], hi[: z.width, :], lo[: z.width, :])
            now[: z.series, :] = now[: z.series, :] + tail[...]

        for i in range(steps):
            now[...] = few(now[...], t[i])
            now[: z.series, :] = now[: z.series, :] + d[i]
            out[i] = now[: z.series, :]

    return call(
        kernel,
        jax.ShapeDtypeStruct((steps, z.series, z.width), F32),
        [*candidates, *left, transition, drive],
        where,
        scratch=[pltpu.VMEM((low, z.width), F32)],
    )


class Tree:
    def __init__(self, segs, size):
        self.segs, self.size = segs, size
        self.depth = size.bit_length() - 1
        if size != 1 << self.depth or self.depth < 3:
            raise ValueError("tm size")

    def root(self, odd, level, group):
        if level == 1:
            return 2 * group + (0 if odd else 1)
        return self.root(odd, level - 1, 2 * group + (1 - group % 2))

    def pairs(self, per_parity):
        return [
            (s * self.size + a, s * self.size + b) for s in range(self.segs) for a, b in per_parity(s % 2)
        ]

    def child_roots(self, odd, level, group):
        return self.root(odd, level - 1, 2 * group), self.root(odd, level - 1, 2 * group + 1)

    def up(self, level):
        def of(odd):
            if level == 1:
                return [(i, i ^ 1) for i in range(self.size) if i % 2 == (1 if odd else 0)]
            found = []
            for g in range(self.size >> level):
                a, b = self.child_roots(odd, level, g)
                if level == self.depth:
                    found += [(a, b), (b, a)]
                else:
                    found.append((a, b) if g % 2 == 0 else (b, a))
            return found

        return self.pairs(of)

    def far(self, bit, seg=None):
        found = []
        for s in range(self.segs) if seg is None else [seg]:
            for i in range(self.size):
                away = i // 2 ^ self.root(0, self.depth - 1, 2 * i // self.size) // 2
                if bit <= away < 2 * bit:
                    found.append((s * self.size + i, s * self.size + (i ^ 2 * bit)))
        return found

    def holds(self, i):
        return i // 2 == self.root(0, self.depth - 1, 2 * i // self.size) // 2

    def root_of(self, odd, level, group):
        for _ in range(level - 1):
            group = 2 * group + 1 - group % 2
        return 2 * group + 1 - odd


def tied(x, after):
    return lax.optimization_barrier((x, after))[0]


def make(mesh):
    segs, size = mesh.shape["seg"], mesh.shape["tm"]
    tree = Tree(segs, size)
    depth = tree.depth
    half = size // 2

    def send(x, pairs):
        return lax.ppermute(x, AXES, pairs)

    def others(level, flip):
        def of(odd):
            found = []
            for g in range(size >> level):
                root = tree.root(odd, level, g)
                a, b = tree.child_roots(odd, level, g)
                found.append((root, (a if root == b else b) ^ flip))
            return found

        return tree.pairs(of)

    def top_and_other(seg, tm, level):
        odd, group = seg % 2, tm >> level
        top = tree.root_of(odd, level, group)
        a, b = (tree.root_of(odd, level - 1, 2 * group + i) for i in (0, 1))
        return top, a + b - top

    def per_device(transition, obs_gain, observed, init_mean, init_factor):
        width, series = transition.shape[1], observed.shape[1]
        chunks = next(n for n in (4, 2, 1) if width % (n * 128) == 0 or n == 1)
        z = Sizes(width, series, chunks)

        def is_even(seg, tm):
            return seg % 2 == 0

        def in_right_half(seg, tm):
            return tm >= half

        own, whole, own_map, drive = local_map(z, is_even, transition, obs_gain, observed)
        first = [send(c, tree.up(1)) for c in own]
        outs = [times_chunk(z, is_even, c, own_map) for c in first]
        back = send(tied(whole, outs), tree.pairs(lambda odd: [(i, i + 1) for i in range(0, size, 2)] if odd else []))
        bits = [1 << i for i in range(depth - 3, -1, -1)]
        start = [init_factor]
        for bit in bits:
            held = start[0] if len(start) == 1 else jnp.concatenate(start)
            start = [held, send(tied(held, outs), tree.far(bit, 0))]
        lefts = {}
        for level in range(2, depth):

            def where(seg, tm, level=level):
                by_rows = seg % 2 == 0 if level == 2 else seg >= 0
                next_rows = tm < half if level == depth - 1 else seg >= 0
                return by_rows, (tm >> level) % 2 == 0, next_rows

            got = [send(c, tree.up(level)) for c in outs]
            outs, mine, lefts[level] = merge(z, where, got, outs)
        crossed, final = [], []
        for k, c in enumerate(outs):
            sent = c if k < AHEAD else tied(c, final[k - AHEAD])
            crossed.append(send(sent, tree.up(depth)))
            final.append(times_chunk(z, in_right_half, crossed[k], mine))
        roots = tree.pairs(lambda odd: [(r, r ^ 1) for r in tree.child_roots(odd, depth, 0)])
        got = [send(c, roots) for c in final]
        left = assemble(z, lambda seg, tm: (seg >= 0, seg % 2 == 1), first, [back])
        halfway = assemble(z, lambda seg, tm: (seg >= 0, seg < 0), crossed)
        got[-1], left, halfway = lax.optimization_barrier((got[-1], left, halfway))

        def beside(seg, tm):
            return tm >= half, tm ^ 1 == tree.root_of(seg % 2, depth - 1, tm // half)

        block = assemble(z, beside, final, got)

        arrived, moved = [], [advance(z, lambda seg, tm: seg >= 0, [*start, init_mean], block)]
        for turn in range(1, segs):
            pairs = [((turn - 1) * size + i, turn * size + i) for i in range(size) if tree.holds(i)]
            arrived.append(send(moved[-1], pairs))

            def where(seg, tm, turn=turn):
                return seg >= turn

            moved.append(advance(z, where, [arrived[-1]], block, moved[-1], turn == segs - 1))

        candidates, cross = [init_mean, *arrived], halfway
        for level in range(depth - 1, 1, -1):

            def where(seg, tm, level=level):
                if level == depth - 1:
                    index = seg
                else:
                    index = (tm == top_and_other(seg, tm, level + 1)[1]).astype(jnp.int32)
                return index, tm >= half, (tm >> level) % 2 == 0

            mine_in, other_in = descend(z, where, candidates, lefts[level], cross)
            candidates, cross = [mine_in, send(other_in, others(level, 0))], None
        candidates.append(send(other_in, others(2, 1)))
        near = tree.pairs(lambda odd: [(tree.root(odd, 2, g), tree.root(odd, 2, g) ^ 1) for g in range(size >> 2)])
        candidates.append(send(mine_in, near))

        kept, given = moved[-1]
        for bit in reversed(bits):
            back_pairs = [(b, a) for a, b in tree.far(bit)]
            came = send(given, back_pairs)

            def where(seg, tm, bit=bit):
                away = tm // 2 ^ tree.root_of(0, depth - 1, tm // half) // 2
                return (away >= bit) & (away < 2 * bit)

            kept = deal(where, kept, came)
            if bit != bits[0]:
                rows = kept.shape[1] // 2
                kept, given = kept[0, :rows], kept[0, rows:]
        ends = kept

        def where(seg, tm):
            top, other = top_and_other(seg, tm, 2)
            index = jnp.where(tm == other, 1, jnp.where(tm == other ^ 1, 2, jnp.where(tm == top, 0, 3)))
            return index, tm % 2 == 1

        return last_steps(z, where, candidates, left, transition, drive), ends

    return per_device


def solution(mesh):
    return jax.shard_map(
        make(mesh),
        mesh=mesh,
        in_specs=(
            P(("seg", "tm"), None, None),
            P(("seg", "tm"), None, None),
            P(("seg", "tm"), None, None),
            P(),
            P("tm", None),
        ),
        out_specs=(P(("seg", "tm"), None, None), P("seg", "tm", None)),
        check_vma=False,
    )
```

profile of v0, /device:TPU:6, one launch (start us, length us, event | category | flops | bytes accessed | tf_op | source)
XLA Modules:
  0.0 98.1 jit_solution(5994571777128142041)
XLA Ops:
  0.6 2.3 %shard_map.68 = (f32[528,128]{1,0:T(8,128)S(1)}, f32[528,128]{1,0:T(8,128)S(1)}, f32[528,128]{1,0:T(8,128)S(1)}, f32[528,128]{1,0:T(8,128)S(1)}, f32[528,512]{1,...) custom-call(bf16[2,512,512]{2,1,0:T(8,128)(2,1)} %refs_7_.1, ...), custom_call_target="tpu_custom_call" | custom-call | tf_op jit(solution)/shard_map/pallas_call | solution.py:102
  2.9 1.3 %collective-permute-start = (f32[528,128]{1,0:T(8,128)S(1)}, f32[528,128]{1,0:T(8,128)S(1)}, u32[]{:S(2)}, u32[]{:S(2)}) collective-permute-start(f32[528,128]{1,0:T(8,128)S(1)} %get-tuple-element.45), channel_id=1, source_target_pairs={{0,1},{2,3},{4,5},{6,7},{9,8},{11,10},{13,12},{15,14},{16,17},{18,... | collective-permute-start | bytes 811016 | tf_op jit(solution)/shard_map/ppermute | solution.py:487
  4.2 1.3 %collective-permute-start.1 = (f32[528,128]{1,0:T(8,128)S(1)}, f32[528,128]{1,0:T(8,128)S(1)}, u32[]{:S(2)}, u32[]{:S(2)}) collective-permute-start(f32[528,128]{1,0:T(8,128)S(1)} %get-tuple-element.49), channel_id=1, source_target_pairs={{0,1},{2,3},{4,5},{6,7},{9,8},{11,10},{13,12},{15,14},{16,17},{18,... | collective-permute-start | bytes 811016 | tf_op jit(solution)/shard_map/ppermute | solution.py:487
  5.5 1.3 %collective-permute-start.2 = (f32[528,128]{1,0:T(8,128)S(1)}, f32[528,128]{1,0:T(8,128)S(1)}, u32[]{:S(2)}, u32[]{:S(2)}) collective-permute-start(f32[528,128]{1,0:T(8,128)S(1)} %get-tuple-element.50), channel_id=1, source_target_pairs={{0,1},{2,3},{4,5},{6,7},{9,8},{11,10},{13,12},{15,14},{16,17},{18,... | collective-permute-start | bytes 811016 | tf_op jit(solution)/shard_map/ppermute | solution.py:487
  6.8 1.3 %collective-permute-start.3 = (f32[528,128]{1,0:T(8,128)S(1)}, f32[528,128]{1,0:T(8,128)S(1)}, u32[]{:S(2)}, u32[]{:S(2)}) collective-permute-start(f32[528,128]{1,0:T(8,128)S(1)} %get-tuple-element.51), channel_id=1, source_target_pairs={{0,1},{2,3},{4,5},{6,7},{9,8},{11,10},{13,12},{15,14},{16,17},{18,... | collective-permute-start | bytes 811016 | tf_op jit(solution)/shard_map/ppermute | solution.py:487
  8.1 3.2 %collective-permute-done.refs_0_ = f32[528,128]{1,0:T(8,128)S(1)} collective-permute-done((f32[528,128]{1,0:T(8,128)S(1)}, f32[528,128]{1,0:T(8,128)S(1)}, u32[]{:S(2)}, u32[]{:S(2)}) %collective-permute-start) | collective-permute-done | bytes 270368 | tf_op jit(solution)/shard_map/ppermute | solution.py:487
  11.7 2.5 %collective-permute-done.1.refs_0_.refs_1_ = f32[528,128]{1,0:T(8,128)S(1)} collective-permute-done((f32[528,128]{1,0:T(8,128)S(1)}, f32[528,128]{1,0:T(8,128)S(1)}, u32[]{:S(2)}, u32[]{:S(2)}) %collective-permute-start.1) | collective-permute-done | bytes 270368 | tf_op jit(solution)/shard_map/ppermute | solution.py:487
  14.6 2.5 %collective-permute-done.2.refs_0_.refs_2_ = f32[528,128]{1,0:T(8,128)S(1)} collective-permute-done((f32[528,128]{1,0:T(8,128)S(1)}, f32[528,128]{1,0:T(8,128)S(1)}, u32[]{:S(2)}, u32[]{:S(2)}) %collective-permute-start.2) | collective-permute-done | bytes 270368 | tf_op jit(solution)/shard_map/ppermute | solution.py:487
  17.5 2.5 %collective-permute-done.3.refs_0_.refs_3_ = f32[528,128]{1,0:T(8,128)S(1)} collective-permute-done((f32[528,128]{1,0:T(8,128)S(1)}, f32[528,128]{1,0:T(8,128)S(1)}, u32[]{:S(2)}, u32[]{:S(2)}) %collective-permute-start.3) | collective-permute-done | bytes 270368 | tf_op jit(solution)/shard_map/ppermute | solution.py:487
  20.4 0.7 collective-permute-start.17
  21.1 3.5 %collective-permute-start.5 = (f32[528,128]{1,0:T(8,128)S(1)}, f32[528,128]{1,0:T(8,128)S(1)}, u32[]{:S(2)}, u32[]{:S(2)}) collective-permute-start(f32[528,128]{1,0:T(8,128)S(1)} %shard_map.69.refs_4_), channel_id=1, source_target_pairs={{1,3},{7,5},{8,10},{14,12},{17,19},{23,21},{24,26},{30,28}} | collective-permute-start | bytes 811016 | tf_op jit(solution)/shard_map/ppermute | solution.py:487
  24.6 1.3 %collective-permute-start.6 = (f32[528,128]{1,0:T(8,128)S(1)}, f32[528,128]{1,0:T(8,128)S(1)}, u32[]{:S(2)}, u32[]{:S(2)}) collective-permute-start(f32[528,128]{1,0:T(8,128)S(1)} %shard_map.70.refs_5_), channel_id=1, source_target_pairs={{1,3},{7,5},{8,10},{14,12},{17,19},{23,21},{24,26},{30,28}} | collective-permute-start | bytes 811016 | tf_op jit(solution)/shard_map/ppermute | solution.py:487
  25.9 1.3 %collective-permute-start.7 = (f32[528,128]{1,0:T(8,128)S(1)}, f32[528,128]{1,0:T(8,128)S(1)}, u32[]{:S(2)}, u32[]{:S(2)}) collective-permute-start(f32[528,128]{1,0:T(8,128)S(1)} %shard_map.71.refs_6_), channel_id=1, source_target_pairs={{1,3},{7,5},{8,10},{14,12},{17,19},{23,21},{24,26},{30,28}} | collective-permute-start | bytes 811016 | tf_op jit(solution)/shard_map/ppermute | solution.py:487
  27.3 1.3 %collective-permute-start.8 = (f32[528,128]{1,0:T(8,128)S(1)}, f32[528,128]{1,0:T(8,128)S(1)}, u32[]{:S(2)}, u32[]{:S(2)}) collective-permute-start(f32[528,128]{1,0:T(8,128)S(1)} %shard_map.72.refs_7_), channel_id=1, source_target_pairs={{1,3},{7,5},{8,10},{14,12},{17,19},{23,21},{24,26},{30,28}} | collective-permute-start | bytes 811016 | tf_op jit(solution)/shard_map/ppermute | solution.py:487
  28.6 2.9 %collective-permute-done.6.refs_1_ = f32[528,128]{1,0:T(8,128)S(1)} collective-permute-done((f32[528,128]{1,0:T(8,128)S(1)}, f32[528,128]{1,0:T(8,128)S(1)}, u32[]{:S(2)}, u32[]{:S(2)}) %collective-permute-start.6) | collective-permute-done | bytes 270368 | tf_op jit(solution)/shard_map/ppermute | solution.py:487
  31.5 2.9 %collective-permute-done.7.refs_2_ = f32[528,128]{1,0:T(8,128)S(1)} collective-permute-done((f32[528,128]{1,0:T(8,128)S(1)}, f32[528,128]{1,0:T(8,128)S(1)}, u32[]{:S(2)}, u32[]{:S(2)}) %collective-permute-start.7) | collective-permute-done | bytes 270368 | tf_op jit(solution)/shard_map/ppermute | solution.py:487
  34.4 2.9 %collective-permute-done.8.refs_3_ = f32[528,128]{1,0:T(8,128)S(1)} collective-permute-done((f32[528,128]{1,0:T(8,128)S(1)}, f32[528,128]{1,0:T(8,128)S(1)}, u32[]{:S(2)}, u32[]{:S(2)}) %collective-permute-start.8) | collective-permute-done | bytes 270368 | tf_op jit(solution)/shard_map/ppermute | solution.py:487
  37.3 1.4 %shard_map.73 = (f32[528,128]{1,0:T(8,128)S(1)}, f32[528,128]{1,0:T(8,128)S(1)}, f32[528,128]{1,0:T(8,128)S(1)}, f32[528,128]{1,0:T(8,128)S(1)}, bf16[528,512]{1...) custom-call(f32[528,128]{1,0:T(8,128)S(1)} %collective-permute-done., ...), custom_call_target="tpu_custom_call" | custom-call | tf_op jit(solution)/shard_map/pallas_call | solution.py:102
  38.7 0.7 collective-permute-start.10
  39.4 0.7 collective-permute-start.9
  40.7 0.7 collective-permute-start.12
  42.0 0.7 collective-permute-start.11
  43.3 0.8 collective-permute-start.16
  44.1 0.7 collective-permute-start.13
  44.8 0.7 collective-permute-start.14
  50.3 0.7 collective-permute-start.19
  51.4 0.7 collective-permute-start.20
  52.1 1.3 %collective-permute-start.24 = (f32[64,512]{1,0:T(8,128)S(1)}, f32[64,512]{1,0:T(8,128)S(1)}, u32[]{:S(2)}, u32[]{:S(2)}) collective-permute-start(f32[64,512]{1,0:T(8,128)S(1)} %get-tuple-element.87), channel_id=1, source_target_pairs={{2,0},{3,1},{4,6},{5,7},{10,8},{11,9},{12,14},{13,15},{18,16},{19,... | collective-permute-start | bytes 393224 | tf_op jit(solution)/shard_map/ppermute | solution.py:487
  53.7 0.8 collective-permute-start.23
  55.2 1.3 %collective-permute-start.21 = (f32[8,512]{1,0:T(8,128)S(1)}, f32[8,512]{1,0:T(8,128)S(1)}, u32[]{:S(2)}, u32[]{:S(2)}) collective-permute-start(f32[8,512]{1,0:T(8,128)S(1)} %get-tuple-element.81), channel_id=1, source_target_pairs={{3,1},{5,7},{10,8},{12,14},{19,17},{21,23},{26,24},{28,30}} | collective-permute-start | bytes 49160 | tf_op jit(solution)/shard_map/ppermute | solution.py:487
  56.5 39.7 %collective-permute-done.21.refs_1_ = f32[8,512]{1,0:T(8,128)S(1)} collective-permute-done((f32[8,512]{1,0:T(8,128)S(1)}, f32[8,512]{1,0:T(8,128)S(1)}, u32[]{:S(2)}, u32[]{:S(2)}) %collective-permute-start.21) | collective-permute-done | bytes 16416 | tf_op jit(solution)/shard_map/ppermute | solution.py:487
  96.2 1.2 %shard_map.85 = f32[2,4,512]{2,1,0:T(4,128)} custom-call(f32[8,512]{1,0:T(8,128)S(1)} %get-tuple-element.80.refs_0_, f32[8,512]{1,0:T(8,128)S(1)} %collective-permute-done.21.refs_1_, f32[8,512]{1,0:T(8,128)S(1)} %collective-permute-done.22.refs_2_, f32[8,512]{1,0:T(8,128)S(1)} %collective-permute-done.23.refs_3_, ...), custom_call_target="tpu_custom_call" | custom-call | tf_op jit(solution)/shard_map/pallas_call | solution.py:102
  (44 shorter events, 10.1 us)
Async XLA Ops:
  2.9 8.4 %collective-permute-start = (f32[528,128]{1,0:T(8,128)S(1)}, f32[528,128]{1,0:T(8,128)S(1)}, u32[]{:S(2)}, u32[]{:S(2)}) collective-permute-start(f32[528,128]{1,0:T(8,128)S(1)} %get-tuple-element.45), channel_id=1, source_target_pairs={{0,1},{2,3},{4,5},{6,7},{9,8},{11,10},{13,12},{15,14},{16,17},{18,... | collective-permute-start | bytes 811016 | tf_op jit(solution)/shard_map/ppermute | solution.py:487
  4.2 10.0 %collective-permute-start.1 = (f32[528,128]{1,0:T(8,128)S(1)}, f32[528,128]{1,0:T(8,128)S(1)}, u32[]{:S(2)}, u32[]{:S(2)}) collective-permute-start(f32[528,128]{1,0:T(8,128)S(1)} %get-tuple-element.49), channel_id=1, source_target_pairs={{0,1},{2,3},{4,5},{6,7},{9,8},{11,10},{13,12},{15,14},{16,17},{18,... | collective-permute-start | bytes 811016 | tf_op jit(solution)/shard_map/ppermute | solution.py:487
  5.5 11.5 %collective-permute-start.2 = (f32[528,128]{1,0:T(8,128)S(1)}, f32[528,128]{1,0:T(8,128)S(1)}, u32[]{:S(2)}, u32[]{:S(2)}) collective-permute-start(f32[528,128]{1,0:T(8,128)S(1)} %get-tuple-element.50), channel_id=1, source_target_pairs={{0,1},{2,3},{4,5},{6,7},{9,8},{11,10},{13,12},{15,14},{16,17},{18,... | collective-permute-start | bytes 811016 | tf_op jit(solution)/shard_map/ppermute | solution.py:487
  6.8 13.1 %collective-permute-start.3 = (f32[528,128]{1,0:T(8,128)S(1)}, f32[528,128]{1,0:T(8,128)S(1)}, u32[]{:S(2)}, u32[]{:S(2)}) collective-permute-start(f32[528,128]{1,0:T(8,128)S(1)} %get-tuple-element.51), channel_id=1, source_target_pairs={{0,1},{2,3},{4,5},{6,7},{9,8},{11,10},{13,12},{15,14},{16,17},{18,... | collective-permute-start | bytes 811016 | tf_op jit(solution)/shard_map/ppermute | solution.py:487
  20.4 26.4 %collective-permute-start.17 = (f32[528,512]{1,0:T(8,128)S(1)}, f32[528,512]{1,0:T(8,128)S(1)}, u32[]{:S(2)}, u32[]{:S(2)}) collective-permute-start(f32[528,512]{1,0:T(8,128)S(1)} %get-tuple-element.63), channel_id=1, source_target_pairs={{8,9},{10,11},{12,13},{14,15},{24,25},{26,27},{28,29},{30,31}} | collective-permute-start | bytes 3244040 | tf_op jit(solution)/shard_map/ppermute | solution.py:487
  21.1 7.4 %collective-permute-start.5 = (f32[528,128]{1,0:T(8,128)S(1)}, f32[528,128]{1,0:T(8,128)S(1)}, u32[]{:S(2)}, u32[]{:S(2)}) collective-permute-start(f32[528,128]{1,0:T(8,128)S(1)} %shard_map.69.refs_4_), channel_id=1, source_target_pairs={{1,3},{7,5},{8,10},{14,12},{17,19},{23,21},{24,26},{30,28}} | collective-permute-start | bytes 811016 | tf_op jit(solution)/shard_map/ppermute | solution.py:487
  24.6 6.8 %collective-permute-start.6 = (f32[528,128]{1,0:T(8,128)S(1)}, f32[528,128]{1,0:T(8,128)S(1)}, u32[]{:S(2)}, u32[]{:S(2)}) collective-permute-start(f32[528,128]{1,0:T(8,128)S(1)} %shard_map.70.refs_5_), channel_id=1, source_target_pairs={{1,3},{7,5},{8,10},{14,12},{17,19},{23,21},{24,26},{30,28}} | collective-permute-start | bytes 811016 | tf_op jit(solution)/shard_map/ppermute | solution.py:487
  25.9 8.4 %collective-permute-start.7 = (f32[528,128]{1,0:T(8,128)S(1)}, f32[528,128]{1,0:T(8,128)S(1)}, u32[]{:S(2)}, u32[]{:S(2)}) collective-permute-start(f32[528,128]{1,0:T(8,128)S(1)} %shard_map.71.refs_6_), channel_id=1, source_target_pairs={{1,3},{7,5},{8,10},{14,12},{17,19},{23,21},{24,26},{30,28}} | collective-permute-start | bytes 811016 | tf_op jit(solution)/shard_map/ppermute | solution.py:487
  27.3 10.0 %collective-permute-start.8 = (f32[528,128]{1,0:T(8,128)S(1)}, f32[528,128]{1,0:T(8,128)S(1)}, u32[]{:S(2)}, u32[]{:S(2)}) collective-permute-start(f32[528,128]{1,0:T(8,128)S(1)} %shard_map.72.refs_7_), channel_id=1, source_target_pairs={{1,3},{7,5},{8,10},{14,12},{17,19},{23,21},{24,26},{30,28}} | collective-permute-start | bytes 811016 | tf_op jit(solution)/shard_map/ppermute | solution.py:487
  38.7 1.4 %collective-permute-start.10 = (f32[528,128]{1,0:T(8,128)S(1)}, f32[528,128]{1,0:T(8,128)S(1)}, u32[]{:S(2)}, u32[]{:S(2)}) collective-permute-start(f32[528,128]{1,0:T(8,128)S(1)} %get-tuple-element.57), channel_id=1, source_target_pairs={{3,5},{5,3},{10,12},{12,10},{19,21},{21,19},{26,28},{28,26}} | collective-permute-start | bytes 811016 | tf_op jit(solution)/shard_map/ppermute | solution.py:487
  39.4 2.0 %collective-permute-start.9 = (f32[528,128]{1,0:T(8,128)S(1)}, f32[528,128]{1,0:T(8,128)S(1)}, u32[]{:S(2)}, u32[]{:S(2)}) collective-permute-start(f32[528,128]{1,0:T(8,128)S(1)} %get-tuple-element.53), channel_id=1, source_target_pairs={{3,5},{5,3},{10,12},{12,10},{19,21},{21,19},{26,28},{28,26}} | collective-permute-start | bytes 811016 | tf_op jit(solution)/shard_map/ppermute | solution.py:487
  40.7 2.0 %collective-permute-start.12 = (f32[528,128]{1,0:T(8,128)S(1)}, f32[528,128]{1,0:T(8,128)S(1)}, u32[]{:S(2)}, u32[]{:S(2)}) collective-permute-start(f32[528,128]{1,0:T(8,128)S(1)} %get-tuple-element.61), channel_id=1, source_target_pairs={{3,5},{5,3},{10,12},{12,10},{19,21},{21,19},{26,28},{28,26}} | collective-permute-start | bytes 811016 | tf_op jit(solution)/shard_map/ppermute | solution.py:487
  42.0 3.5 %collective-permute-start.11 = (f32[528,128]{1,0:T(8,128)S(1)}, f32[528,128]{1,0:T(8,128)S(1)}, u32[]{:S(2)}, u32[]{:S(2)}) collective-permute-start(f32[528,128]{1,0:T(8,128)S(1)} %get-tuple-element.59), channel_id=1, source_target_pairs={{3,5},{5,3},{10,12},{12,10},{19,21},{21,19},{26,28},{28,26}} | collective-permute-start | bytes 811016 | tf_op jit(solution)/shard_map/ppermute | solution.py:487
  43.3 3.5 %copy-start.1 = (f32[64,512]{1,0:T(8,128)S(1)}, f32[64,512]{1,0:T(8,128)}, u32[]{:S(2)}) copy-start(f32[64,512]{1,0:T(8,128)} %refs_0_.4) | copy-start | bytes 393220
  43.3 4.7 %collective-permute-start.16 = (f32[528,128]{1,0:T(8,128)S(1)}, f32[528,128]{1,0:T(8,128)S(1)}, u32[]{:S(2)}, u32[]{:S(2)}) collective-permute-start(f32[528,128]{1,0:T(8,128)S(1)} %shard_map.77.refs_3_), channel_id=1, source_target_pairs={{3,2},{5,4},{10,11},{12,13},{19,18},{21,20},{26,27},{28,29}} | collective-permute-start | bytes 811016 | tf_op jit(solution)/shard_map/ppermute | solution.py:487
  44.1 3.9 %collective-permute-start.13 = (f32[528,128]{1,0:T(8,128)S(1)}, f32[528,128]{1,0:T(8,128)S(1)}, u32[]{:S(2)}, u32[]{:S(2)}) collective-permute-start(f32[528,128]{1,0:T(8,128)S(1)} %shard_map.74.refs_0_), channel_id=1, source_target_pairs={{3,2},{5,4},{10,11},{12,13},{19,18},{21,20},{26,27},{28,29}} | collective-permute-start | bytes 811016 | tf_op jit(solution)/shard_map/ppermute | solution.py:487
  44.8 3.3 %collective-permute-start.14 = (f32[528,128]{1,0:T(8,128)S(1)}, f32[528,128]{1,0:T(8,128)S(1)}, u32[]{:S(2)}, u32[]{:S(2)}) collective-permute-start(f32[528,128]{1,0:T(8,128)S(1)} %shard_map.75.refs_1_), channel_id=1, source_target_pairs={{3,2},{5,4},{10,11},{12,13},{19,18},{21,20},{26,27},{28,29}} | collective-permute-start | bytes 811016 | tf_op jit(solution)/shard_map/ppermute | solution.py:487
  46.1 2.0 %collective-permute-start.15 = (f32[528,128]{1,0:T(8,128)S(1)}, f32[528,128]{1,0:T(8,128)S(1)}, u32[]{:S(2)}, u32[]{:S(2)}) collective-permute-start(f32[528,128]{1,0:T(8,128)S(1)} %shard_map.76.refs_2_), channel_id=1, source_target_pairs={{3,2},{5,4},{10,11},{12,13},{19,18},{21,20},{26,27},{28,29}} | collective-permute-start | bytes 811016 | tf_op jit(solution)/shard_map/ppermute | solution.py:487
  46.8 1.6 %collective-permute-start.4 = (f32[64,512]{1,0:T(8,128)S(1)}, f32[64,512]{1,0:T(8,128)S(1)}, u32[]{:S(2)}, u32[]{:S(2)}) collective-permute-start(f32[64,512]{1,0:T(8,128)S(1)} %copy-done.1), channel_id=1, source_target_pairs={{0,2},{1,3},{6,4},{7,5}} | collective-permute-start | bytes 393224 | tf_op jit(solution)/shard_map/ppermute | solution.py:487
  48.1 0.7 copy-start.2
  49.2 0.7 collective-permute-start.18
  50.3 0.7 collective-permute-start.19
  51.4 0.7 collective-permute-start.20
  52.1 45.3 %collective-permute-start.24 = (f32[64,512]{1,0:T(8,128)S(1)}, f32[64,512]{1,0:T(8,128)S(1)}, u32[]{:S(2)}, u32[]{:S(2)}) collective-permute-start(f32[64,512]{1,0:T(8,128)S(1)} %get-tuple-element.87), channel_id=1, source_target_pairs={{2,0},{3,1},{4,6},{5,7},{10,8},{11,9},{12,14},{13,15},{18,16},{19,... | collective-permute-start | bytes 393224 | tf_op jit(solution)/shard_map/ppermute | solution.py:487
  53.4 42.7 %copy-start = (bf16[2,512,512]{2,1,0:T(8,128)(2,1)S(1)}, bf16[2,512,512]{2,1,0:T(8,128)(2,1)}, u32[]{:S(2)}) copy-start(bf16[2,512,512]{2,1,0:T(8,128)(2,1)} %refs_7_.1) | copy-start | bytes 3145732
  53.7 2.8 %collective-permute-start.23 = (f32[8,512]{1,0:T(8,128)S(1)}, f32[8,512]{1,0:T(8,128)S(1)}, u32[]{:S(2)}, u32[]{:S(2)}) collective-permute-start(f32[8,512]{1,0:T(8,128)S(1)} %get-tuple-element.80.refs_0_), channel_id=1, source_target_pairs={{3,2},{5,4},{10,11},{12,13},{19,18},{21,20},{26,27},{28,29}} | collective-permute-start | bytes 49160 | tf_op jit(solution)/shard_map/ppermute | solution.py:487
  54.5 2.0 %collective-permute-start.22 = (f32[8,512]{1,0:T(8,128)S(1)}, f32[8,512]{1,0:T(8,128)S(1)}, u32[]{:S(2)}, u32[]{:S(2)}) collective-permute-start(f32[8,512]{1,0:T(8,128)S(1)} %get-tuple-element.81), channel_id=1, source_target_pairs={{3,0},{5,6},{10,9},{12,15},{19,16},{21,22},{26,25},{28,31}} | collective-permute-start | bytes 49160 | tf_op jit(solution)/shard_map/ppermute | solution.py:487
  55.2 41.0 %collective-permute-start.21 = (f32[8,512]{1,0:T(8,128)S(1)}, f32[8,512]{1,0:T(8,128)S(1)}, u32[]{:S(2)}, u32[]{:S(2)}) collective-permute-start(f32[8,512]{1,0:T(8,128)S(1)} %get-tuple-element.81), channel_id=1, source_target_pairs={{3,1},{5,7},{10,8},{12,14},{19,17},{21,23},{26,24},{28,30}} | collective-permute-start | bytes 49160 | tf_op jit(solution)/shard_map/ppermute | solution.py:487
where the time goes:
time: 98.7 us; the launch traced here: 98.1 us
  waiting for transfers between devices  59 us (60%)
  starting transfers between devices  25.6 us (26%)
  Pallas kernels  12 us (12%)
  between operations  1.1 us (1%)
    ppermute x25, waiting for transfers between devices, send(): return lax.ppermute(x, AXES, pairs)  59 us
    ppermute x25, starting transfers between devices, send(): return lax.ppermute(x, AXES, pairs)  25.6 us
    pallas_call x20, Pallas kernels, call(): pl.pallas_call(body, out_shape=outs, in_specs=in_specs, out_specs=jax.tre...  12 us
  transfers between devices with their start and end apart: 25, of which 8 were waited for; matrix products, arithmetic and copies ran while one was open for 0% of the time, Pallas kernels for 8%

commit v1 on v0

--- a/solution.py
+++ b/solution.py
@@ -9,7 +9,6 @@
 BF16 = jnp.bfloat16
 AXES = ("seg", "tm")
 GRANT = 10 * 1024 * 1024
-AHEAD = 2
 
 
 def halves(x):
@@ -130,7 +129,11 @@
 def local_map(z, where, transition, gain, observed):
     steps = transition.shape[0]
 
-    def kernel(by_rows, t_hbm, g_hbm, o_hbm, *rest):
+    def kernel(flag, *refs):
+        by_rows, active = flag
+        pl.when(active)(lambda: run(by_rows, *refs))
+
+    def run(by_rows, t_hbm, g_hbm, o_hbm, *rest):
         chunks, (whole, hi, lo, tail, drive) = rest[: z.chunks], rest[z.chunks : z.chunks + 5]
         t, g, o, sems = rest[z.chunks + 5 :]
         copies = [
@@ -184,39 +187,66 @@
     return res[:n], res[n], tuple(res[n + 1 : n + 4]), res[n + 4]
 
 
+def quarter(z, ref, k):
+    return ref.at[pl.ds(k * z.buf, z.buf)]
+
+
+def split_parts(z, refs):
+    return [quarter(z, ref, k) for ref in refs for k in range(ref.shape[0] // z.buf)]
+
+
 def times_chunk(z, where, chunk, own):
-    def kernel(by_rows, got, own_hi, own_lo, own_tail, out, left):
+    count = chunk.shape[0] // z.buf
+    span = count * z.part
+
+    def kernel(by_rows, got, own_hi, own_lo, own_tail, *rest):
+        outs, (left, right) = rest[:count], rest[count:]
+        gots = split_parts(z, [got])
+
         @pl.when(by_rows)
         def _():
-            left[z.part :, :] = jnp.zeros((left.shape[0] - z.part, z.width), F32)
+            left[span:, :] = jnp.zeros((left.shape[0] - span, z.width), F32)
             for j in range(z.chunks):
                 cols = slice(j * z.part, (j + 1) * z.part)
-                left[: z.part, cols] = got[j * z.part : (j + 1) * z.part, :]
-                left[z.part : z.part + z.series, cols] = got[z.width + j * z.series : z.width + (j + 1) * z.series, :]
+                for q, part in enumerate(gots):
+                    left[q * z.part : (q + 1) * z.part, cols] = part[j * z.part : (j + 1) * z.part, :]
+                left[span : span + z.series, cols] = gots[0][z.width + j * z.series : z.width + (j + 1) * z.series, :]
             l_hi, l_lo = halves(left[...])
             res = dot3(l_hi, l_lo, own_hi[: z.width, :], own_lo[: z.width, :])
-            put_rows(z, out, res[: z.part], res[z.part : z.part + z.series] + own_tail[...])
+            for q, out in enumerate(outs):
+                put_rows(z, out, res[q * z.part : (q + 1) * z.part], res[span : span + z.series] + own_tail[...])
 
         @pl.when(jnp.logical_not(by_rows))
         def _():
-            r_hi, r_lo = halves(got[: z.width, :])
+            for q, part in enumerate(gots):
+                right[:, q * z.part : (q + 1) * z.part] = part[: z.width + z.series, :]
+            r_hi, r_lo = halves(right[: z.width, :])
             res = dot3(own_hi[...], own_lo[...], r_hi, r_lo)
-            out[z.width :, :] = jnp.zeros((z.buf - z.width, z.part), F32)
-            put_cols(z, out, res[: z.width], res[z.width : z.width + z.series] + got[z.width : z.width + z.series, :])
+            low = res[z.width : z.width + z.series] + right[z.width : z.width + z.series, :]
+            for q, out in enumerate(outs):
+                cols = slice(q * z.part, (q + 1) * z.part)
+                out[z.width :, :] = jnp.zeros((z.buf - z.width, z.part), F32)
+                put_cols(z, out, res[: z.width, cols], low[:, cols])
 
     return call(
-        kernel, shape(z.buf, z.part), [chunk, *own], where, scratch=[pltpu.VMEM((z.part + z.low, z.width), F32)]
+        kernel,
+        [shape(z.buf, z.part)] * count,
+        [chunk, *own],
+        where,
+        scratch=[pltpu.VMEM((span + z.low, z.width), F32), pltpu.VMEM((z.width + z.series, span), F32)],
     )
 
 
-def merge(z, where, got, own):
+def merge(z, where, got, own, count=None):
+    sent = count or z.chunks
+
     def kernel(flag, *refs):
         by_rows, got_left, next_rows = flag
         n = z.chunks
         gots, owns = refs[:n], refs[n : 2 * n]
-        outs = refs[2 * n : 3 * n]
-        hi, lo, tail, left_hi, left_lo, left_tail = refs[3 * n : 3 * n + 6]
-        a, b, c = refs[3 * n + 6 :]
+        outs = split_parts(z, refs[2 * n : 2 * n + sent])
+        hi, lo, tail, left_hi, left_lo, left_tail = refs[2 * n + sent : 2 * n + sent + 6]
+        a, b, c = refs[2 * n + sent + 6 :]
         clear_low(z, a)
         clear_low(z, b)
 
@@ -241,13 +271,12 @@
 
     res = call(
         kernel,
-        [shape(z.buf, z.part)] * z.chunks + map_shapes(z) * 2,
+        [shape(z.chunks // sent * z.buf, z.part)] * sent + map_shapes(z) * 2,
         list(got) + list(own),
         where,
         scratch=[pltpu.VMEM((z.tall, z.width), F32)] * 3,
     )
-    n = z.chunks
-    return res[:n], tuple(res[n : n + 3]), tuple(res[n + 3 :])
+    return res[:sent], tuple(res[sent : sent + 3]), tuple(res[sent + 3 :])
 
 
 def assemble(z, where, chunks, others=None):
@@ -255,8 +284,8 @@
 
     def kernel(flag, *refs):
         by_rows, swap = flag
-        n = z.chunks
-        bufs, rest = refs[:n], refs[n : n + len(extra)]
+        n = len(chunks)
+        bufs, rest = split_parts(z, refs[:n]), refs[n : n + len(extra)]
         hi, lo, tail, full = refs[n + len(extra) :]
         clear_low(z, full)
         if not extra:
@@ -391,14 +420,14 @@
     )
 
 
-def last_steps(z, where, candidates, left, transition, drive):
+def last_steps(z, where, candidates, left, transition, drives):
     steps = transition.shape[0]
     m = len(candidates)
     low = padded(z.series)
 
     def kernel(flag, *refs):
-        index, through = flag
-        hi, lo, tail, t, d, out, now = refs[m:]
+        index, through, second = flag
+        hi, lo, tail, t, d0, d1, out, now = refs[m:]
         load_choice(z, index, refs[:m], now)
 
         @pl.when(through)
@@ -408,13 +437,13 @@
 
         for i in range(steps):
             now[...] = few(now[...], t[i])
-            now[: z.series, :] = now[: z.series, :] + d[i]
+            now[: z.series, :] = now[: z.series, :] + jnp.where(second, d1[i], d0[i])
             out[i] = now[: z.series, :]
 
     return call(
         kernel,
         jax.ShapeDtypeStruct((steps, z.series, z.width), F32),
-        [*candidates, *left, transition, drive],
+        [*candidates, *left, transition, *drives],
         where,
         scratch=[pltpu.VMEM((low, z.width), F32)],
     )
@@ -514,9 +543,19 @@
         def in_right_half(seg, tm):
             return tm >= half
 
-        own, whole, own_map, drive = local_map(z, is_even, transition, obs_gain, observed)
+        def sends(seg, tm):
+            return seg % 2 == 0, (seg + tm) % 2 == 0
+
+        def receives(seg, tm):
+            return seg % 2 == 0, (seg + tm) % 2 == 1
+
+        def one_chunk(c):
+            return times_chunk(z, is_even, c, own_map)[0]
+
+        own, _, _, early = local_map(z, sends, transition, obs_gain, observed)
         first = [send(c, tree.up(1)) for c in own]
-        outs = [times_chunk(z, is_even, c, own_map) for c in first]
+        _, whole, own_map, late = local_map(z, receives, transition, obs_gain, observed)
+        outs = [one_chunk(c) for c in first]
         back = send(tied(whole, outs), tree.pairs(lambda odd: [(i, i + 1) for i in range(0, size, 2)] if odd else []))
         bits = [1 << i for i in range(depth - 3, -1, -1)]
         start = [init_factor]
@@ -532,12 +571,10 @@
                 return by_rows, (tm >> level) % 2 == 0, next_rows
 
             got = [send(c, tree.up(level)) for c in outs]
-            outs, mine, lefts[level] = merge(z, where, got, outs)
-        crossed, final = [], []
-        for k, c in enumerate(outs):
-            sent = c if k < AHEAD else tied(c, final[k - AHEAD])
-            crossed.append(send(sent, tree.up(depth)))
-            final.append(times_chunk(z, in_right_half, crossed[k], mine))
+            count = min(2, chunks) if level == depth - 1 else None
+            outs, mine, lefts[level] = merge(z, where, got, outs, count)
+        crossed = [send(c, tree.up(depth)) for c in outs]
+        final = [part for c in crossed for part in times_chunk(z, in_right_half, c, mine)]
         roots = tree.pairs(lambda odd: [(r, r ^ 1) for r in tree.child_roots(odd, depth, 0)])
         got = [send(c, roots) for c in final]
         left = assemble(z, lambda seg, tm: (seg >= 0, seg % 2 == 1), first, [back])
@@ -593,9 +630,9 @@
         def where(seg, tm):
             top, other = top_and_other(seg, tm, 2)
             index = jnp.where(tm == other, 1, jnp.where(tm == other ^ 1, 2, jnp.where(tm == top, 0, 3)))
-            return index, tm % 2 == 1
-
-        return last_steps(z, where, candidates, left, transition, drive), ends
+            return index, tm % 2 == 1, (seg + tm) % 2 == 1
+
+        return last_steps(z, where, candidates, left, transition, (early, late)), ends
 
     return per_device
 

time: 98.7 us -> 94.6 us (0.958)
  waiting for transfers between devices: 59 us -> 55.1 us
  Pallas kernels: 12 us -> 13.3 us
  starting transfers between devices: 25.6 us -> 24.3 us
    ppermute x25 -> x23, waiting for transfers between devices: 59 us -> 55.1 us  [send(): return lax.ppermute(x, AXES, pairs)]
    ppermute x25 -> x23, starting transfers between devices: 25.6 us -> 24.3 us  [send(): return lax.ppermute(x, AXES, pairs)]
    pallas_call x20 -> x19, Pallas kernels: 12 us -> 13.3 us  [call(): pl.pallas_call(body, out_shape=outs, in_specs=in_specs, out_specs=jax.tre...]
  transfers between devices with their start and end apart: 25 -> 23, of which waited for: 8 -> 7; matrix products, arithmetic and copies ran while one was open for 0% -> 0% of each run, Pallas kernels for 8% -> 10%
where the time goes in v1:
time: 94.6 us; the launch traced here: 94 us
  waiting for transfers between devices  55.1 us (58%)
  starting transfers between devices  24.3 us (26%)
  Pallas kernels  13.3 us (14%)
  between operations  1.08 us (1%)
    ppermute x23, waiting for transfers between devices, send(): return lax.ppermute(x, AXES, pairs)  55.1 us
    ppermute x23, starting transfers between devices, send(): return lax.ppermute(x, AXES, pairs)  24.3 us
    pallas_call x19, Pallas kernels, call(): pl.pallas_call(body, out_shape=outs, in_specs=in_specs, out_specs=jax.tre...  13.3 us
  transfers between devices with their start and end apart: 23, of which 7 were waited for; matrix products, arithmetic and copies ran while one was open for 0% of the time, Pallas kernels for 10%

profile of v1, /device:TPU:6, one launch (start us, length us, event | category | flops | bytes accessed | tf_op | source)
XLA Modules:
  0.0 94.0 jit_solution(4655124870966143220)
XLA Ops:
  0.6 1.4 %shard_map.68 = (f32[528,128]{1,0:T(8,128)S(1)}, f32[528,128]{1,0:T(8,128)S(1)}, f32[528,128]{1,0:T(8,128)S(1)}, f32[528,128]{1,0:T(8,128)S(1)}, f32[528,512]{1,...) custom-call(bf16[2,512,512]{2,1,0:T(8,128)(2,1)} %refs_7_.1, ...), custom_call_target="tpu_custom_call" | custom-call | tf_op jit(solution)/shard_map/pallas_call | solution.py:101
  2.0 1.3 %collective-permute-start = (f32[528,128]{1,0:T(8,128)S(1)}, f32[528,128]{1,0:T(8,128)S(1)}, u32[]{:S(2)}, u32[]{:S(2)}) collective-permute-start(f32[528,128]{1,0:T(8,128)S(1)} %get-tuple-element.46), channel_id=1, source_target_pairs={{0,1},{2,3},{4,5},{6,7},{9,8},{11,10},{13,12},{15,14},{16,17},{18,... | collective-permute-start | bytes 811016 | tf_op jit(solution)/shard_map/ppermute | solution.py:516
  3.3 1.3 %collective-permute-start.1 = (f32[528,128]{1,0:T(8,128)S(1)}, f32[528,128]{1,0:T(8,128)S(1)}, u32[]{:S(2)}, u32[]{:S(2)}) collective-permute-start(f32[528,128]{1,0:T(8,128)S(1)} %get-tuple-element.50), channel_id=1, source_target_pairs={{0,1},{2,3},{4,5},{6,7},{9,8},{11,10},{13,12},{15,14},{16,17},{18,... | collective-permute-start | bytes 811016 | tf_op jit(solution)/shard_map/ppermute | solution.py:516
  4.6 1.3 %collective-permute-start.2 = (f32[528,128]{1,0:T(8,128)S(1)}, f32[528,128]{1,0:T(8,128)S(1)}, u32[]{:S(2)}, u32[]{:S(2)}) collective-permute-start(f32[528,128]{1,0:T(8,128)S(1)} %get-tuple-element.51), channel_id=1, source_target_pairs={{0,1},{2,3},{4,5},{6,7},{9,8},{11,10},{13,12},{15,14},{16,17},{18,... | collective-permute-start | bytes 811016 | tf_op jit(solution)/shard_map/ppermute | solution.py:516
  5.9 1.3 %collective-permute-start.3 = (f32[528,128]{1,0:T(8,128)S(1)}, f32[528,128]{1,0:T(8,128)S(1)}, u32[]{:S(2)}, u32[]{:S(2)}) collective-permute-start(f32[528,128]{1,0:T(8,128)S(1)} %get-tuple-element.52), channel_id=1, source_target_pairs={{0,1},{2,3},{4,5},{6,7},{9,8},{11,10},{13,12},{15,14},{16,17},{18,... | collective-permute-start | bytes 811016 | tf_op jit(solution)/shard_map/ppermute | solution.py:516
  7.2 3.3 %shard_map.69 = (f32[528,128]{1,0:T(8,128)}, f32[528,128]{1,0:T(8,128)}, f32[528,128]{1,0:T(8,128)}, f32[528,128]{1,0:T(8,128)}, f32[528,512]{1,0:T(8,128)S(1)},...) custom-call(bf16[2,512,512]{2,1,0:T(8,128)(2,1)} %refs_7_.1, ...), custom_call_target="tpu_custom_call" | custom-call | tf_op jit(solution)/shard_map/pallas_call | solution.py:101
  11.0 2.4 %collective-permute-done.1.refs_0_.refs_1_ = f32[528,128]{1,0:T(8,128)S(1)} collective-permute-done((f32[528,128]{1,0:T(8,128)S(1)}, f32[528,128]{1,0:T(8,128)S(1)}, u32[]{:S(2)}, u32[]{:S(2)}) %collective-permute-start.1) | collective-permute-done | bytes 270368 | tf_op jit(solution)/shard_map/ppermute | solution.py:516
  13.8 2.5 %collective-permute-done.2.refs_0_.refs_2_ = f32[528,128]{1,0:T(8,128)S(1)} collective-permute-done((f32[528,128]{1,0:T(8,128)S(1)}, f32[528,128]{1,0:T(8,128)S(1)}, u32[]{:S(2)}, u32[]{:S(2)}) %collective-permute-start.2) | collective-permute-done | bytes 270368 | tf_op jit(solution)/shard_map/ppermute | solution.py:516
  16.7 2.5 %collective-permute-done.3.refs_0_.refs_3_ = f32[528,128]{1,0:T(8,128)S(1)} collective-permute-done((f32[528,128]{1,0:T(8,128)S(1)}, f32[528,128]{1,0:T(8,128)S(1)}, u32[]{:S(2)}, u32[]{:S(2)}) %collective-permute-start.3) | collective-permute-done | bytes 270368 | tf_op jit(solution)/shard_map/ppermute | solution.py:516
  19.6 0.7 collective-permute-start.15
  20.4 3.5 %collective-permute-start.5 = (f32[528,128]{1,0:T(8,128)S(1)}, f32[528,128]{1,0:T(8,128)S(1)}, u32[]{:S(2)}, u32[]{:S(2)}) collective-permute-start(f32[528,128]{1,0:T(8,128)S(1)} %shard_map.70.refs_4_), channel_id=1, source_target_pairs={{1,3},{7,5},{8,10},{14,12},{17,19},{23,21},{24,26},{30,28}} | collective-permute-start | bytes 811016 | tf_op jit(solution)/shard_map/ppermute | solution.py:516
  23.9 1.3 %collective-permute-start.6 = (f32[528,128]{1,0:T(8,128)S(1)}, f32[528,128]{1,0:T(8,128)S(1)}, u32[]{:S(2)}, u32[]{:S(2)}) collective-permute-start(f32[528,128]{1,0:T(8,128)S(1)} %shard_map.71.refs_5_), channel_id=1, source_target_pairs={{1,3},{7,5},{8,10},{14,12},{17,19},{23,21},{24,26},{30,28}} | collective-permute-start | bytes 811016 | tf_op jit(solution)/shard_map/ppermute | solution.py:516
  25.2 1.3 %collective-permute-start.7 = (f32[528,128]{1,0:T(8,128)S(1)}, f32[528,128]{1,0:T(8,128)S(1)}, u32[]{:S(2)}, u32[]{:S(2)}) collective-permute-start(f32[528,128]{1,0:T(8,128)S(1)} %shard_map.72.refs_6_), channel_id=1, source_target_pairs={{1,3},{7,5},{8,10},{14,12},{17,19},{23,21},{24,26},{30,28}} | collective-permute-start | bytes 811016 | tf_op jit(solution)/shard_map/ppermute | solution.py:516
  26.5 1.3 %collective-permute-start.8 = (f32[528,128]{1,0:T(8,128)S(1)}, f32[528,128]{1,0:T(8,128)S(1)}, u32[]{:S(2)}, u32[]{:S(2)}) collective-permute-start(f32[528,128]{1,0:T(8,128)S(1)} %shard_map.73.refs_7_), channel_id=1, source_target_pairs={{1,3},{7,5},{8,10},{14,12},{17,19},{23,21},{24,26},{30,28}} | collective-permute-start | bytes 811016 | tf_op jit(solution)/shard_map/ppermute | solution.py:516
  27.8 2.9 %collective-permute-done.6.refs_1_ = f32[528,128]{1,0:T(8,128)S(1)} collective-permute-done((f32[528,128]{1,0:T(8,128)S(1)}, f32[528,128]{1,0:T(8,128)S(1)}, u32[]{:S(2)}, u32[]{:S(2)}) %collective-permute-start.6) | collective-permute-done | bytes 270368 | tf_op jit(solution)/shard_map/ppermute | solution.py:516
  30.7 2.9 %collective-permute-done.7.refs_2_ = f32[528,128]{1,0:T(8,128)S(1)} collective-permute-done((f32[528,128]{1,0:T(8,128)S(1)}, f32[528,128]{1,0:T(8,128)S(1)}, u32[]{:S(2)}, u32[]{:S(2)}) %collective-permute-start.7) | collective-permute-done | bytes 270368 | tf_op jit(solution)/shard_map/ppermute | solution.py:516
  33.6 2.9 %collective-permute-done.8.refs_3_ = f32[528,128]{1,0:T(8,128)S(1)} collective-permute-done((f32[528,128]{1,0:T(8,128)S(1)}, f32[528,128]{1,0:T(8,128)S(1)}, u32[]{:S(2)}, u32[]{:S(2)}) %collective-permute-start.8) | collective-permute-done | bytes 270368 | tf_op jit(solution)/shard_map/ppermute | solution.py:516
  36.5 1.4 %shard_map.74 = (f32[1056,128]{1,0:T(8,128)S(1)}, f32[1056,128]{1,0:T(8,128)S(1)}, bf16[528,512]{1,0:T(8,128)(2,1)S(1)}, bf16[528,512]{1,0:T(8,128)(2,1)S(1)}, f...) custom-call(f32[528,128]{1,0:T(8,128)S(1)} %collective-permute-done.5.r, ...), custom_call_target="tpu_custom_call" | custom-call | tf_op jit(solution)/shard_map/pallas_call | solution.py:101
  38.0 0.7 collective-permute-start.10
  38.7 0.7 collective-permute-start.9
  40.0 0.8 collective-permute-start.14
  41.4 0.7 collective-permute-start.11
  42.1 0.7 collective-permute-start.12
  42.8 0.7 collective-permute-start.13
  45.9 0.7 collective-permute-start.16
  47.0 0.7 collective-permute-start.17
  48.1 0.7 collective-permute-start.18
  48.8 1.3 %collective-permute-start.22 = (f32[64,512]{1,0:T(8,128)S(1)}, f32[64,512]{1,0:T(8,128)S(1)}, u32[]{:S(2)}, u32[]{:S(2)}) collective-permute-start(f32[64,512]{1,0:T(8,128)S(1)} %get-tuple-element.89), channel_id=1, source_target_pairs={{2,0},{3,1},{4,6},{5,7},{10,8},{11,9},{12,14},{13,15},{18,16},{19,... | collective-permute-start | bytes 393224 | tf_op jit(solution)/shard_map/ppermute | solution.py:516
  50.4 0.8 collective-permute-start.21
  51.9 1.3 %collective-permute-start.19 = (f32[8,512]{1,0:T(8,128)S(1)}, f32[8,512]{1,0:T(8,128)S(1)}, u32[]{:S(2)}, u32[]{:S(2)}) collective-permute-start(f32[8,512]{1,0:T(8,128)S(1)} %get-tuple-element.82), channel_id=1, source_target_pairs={{3,1},{5,7},{10,8},{12,14},{19,17},{21,23},{26,24},{28,30}} | collective-permute-start | bytes 49160 | tf_op jit(solution)/shard_map/ppermute | solution.py:516
  53.2 38.9 %collective-permute-done.19.refs_1_ = f32[8,512]{1,0:T(8,128)S(1)} collective-permute-done((f32[8,512]{1,0:T(8,128)S(1)}, f32[8,512]{1,0:T(8,128)S(1)}, u32[]{:S(2)}, u32[]{:S(2)}) %collective-permute-start.19) | collective-permute-done | bytes 16416 | tf_op jit(solution)/shard_map/ppermute | solution.py:516
  92.1 1.2 %shard_map.84 = f32[2,4,512]{2,1,0:T(4,128)} custom-call(f32[8,512]{1,0:T(8,128)S(1)} %get-tuple-element.81.refs_0_, f32[8,512]{1,0:T(8,128)S(1)} %collective-permute-done.19.refs_1_, f32[8,512]{1,0:T(8,128)S(1)} %collective-permute-done.20.refs_2_, f32[8,512]{1,0:T(8,128)S(1)} %collective-permute-done.21.refs_3_, ...), custom_call_target="tpu_custom_call" | custom-call | tf_op jit(solution)/shard_map/pallas_call | solution.py:101
  (39 shorter events, 7.6 us)
Async XLA Ops:
  2.0 8.5 %collective-permute-start = (f32[528,128]{1,0:T(8,128)S(1)}, f32[528,128]{1,0:T(8,128)S(1)}, u32[]{:S(2)}, u32[]{:S(2)}) collective-permute-start(f32[528,128]{1,0:T(8,128)S(1)} %get-tuple-element.46), channel_id=1, source_target_pairs={{0,1},{2,3},{4,5},{6,7},{9,8},{11,10},{13,12},{15,14},{16,17},{18,... | collective-permute-start | bytes 811016 | tf_op jit(solution)/shard_map/ppermute | solution.py:516
  3.3 10.1 %collective-permute-start.1 = (f32[528,128]{1,0:T(8,128)S(1)}, f32[528,128]{1,0:T(8,128)S(1)}, u32[]{:S(2)}, u32[]{:S(2)}) collective-permute-start(f32[528,128]{1,0:T(8,128)S(1)} %get-tuple-element.50), channel_id=1, source_target_pairs={{0,1},{2,3},{4,5},{6,7},{9,8},{11,10},{13,12},{15,14},{16,17},{18,... | collective-permute-start | bytes 811016 | tf_op jit(solution)/shard_map/ppermute | solution.py:516
  4.6 11.7 %collective-permute-start.2 = (f32[528,128]{1,0:T(8,128)S(1)}, f32[528,128]{1,0:T(8,128)S(1)}, u32[]{:S(2)}, u32[]{:S(2)}) collective-permute-start(f32[528,128]{1,0:T(8,128)S(1)} %get-tuple-element.51), channel_id=1, source_target_pairs={{0,1},{2,3},{4,5},{6,7},{9,8},{11,10},{13,12},{15,14},{16,17},{18,... | collective-permute-start | bytes 811016 | tf_op jit(solution)/shard_map/ppermute | solution.py:516
  5.9 13.3 %collective-permute-start.3 = (f32[528,128]{1,0:T(8,128)S(1)}, f32[528,128]{1,0:T(8,128)S(1)}, u32[]{:S(2)}, u32[]{:S(2)}) collective-permute-start(f32[528,128]{1,0:T(8,128)S(1)} %get-tuple-element.52), channel_id=1, source_target_pairs={{0,1},{2,3},{4,5},{6,7},{9,8},{11,10},{13,12},{15,14},{16,17},{18,... | collective-permute-start | bytes 811016 | tf_op jit(solution)/shard_map/ppermute | solution.py:516
  19.6 23.9 %collective-permute-start.15 = (f32[528,512]{1,0:T(8,128)S(1)}, f32[528,512]{1,0:T(8,128)S(1)}, u32[]{:S(2)}, u32[]{:S(2)}) collective-permute-start(f32[528,512]{1,0:T(8,128)S(1)} %get-tuple-element.64), channel_id=1, source_target_pairs={{8,9},{10,11},{12,13},{14,15},{24,25},{26,27},{28,29},{30,31}} | collective-permute-start | bytes 3244040 | tf_op jit(solution)/shard_map/ppermute | solution.py:516
  20.4 7.5 %collective-permute-start.5 = (f32[528,128]{1,0:T(8,128)S(1)}, f32[528,128]{1,0:T(8,128)S(1)}, u32[]{:S(2)}, u32[]{:S(2)}) collective-permute-start(f32[528,128]{1,0:T(8,128)S(1)} %shard_map.70.refs_4_), channel_id=1, source_target_pairs={{1,3},{7,5},{8,10},{14,12},{17,19},{23,21},{24,26},{30,28}} | collective-permute-start | bytes 811016 | tf_op jit(solution)/shard_map/ppermute | solution.py:516
  23.9 6.8 %collective-permute-start.6 = (f32[528,128]{1,0:T(8,128)S(1)}, f32[528,128]{1,0:T(8,128)S(1)}, u32[]{:S(2)}, u32[]{:S(2)}) collective-permute-start(f32[528,128]{1,0:T(8,128)S(1)} %shard_map.71.refs_5_), channel_id=1, source_target_pairs={{1,3},{7,5},{8,10},{14,12},{17,19},{23,21},{24,26},{30,28}} | collective-permute-start | bytes 811016 | tf_op jit(solution)/shard_map/ppermute | solution.py:516
  25.2 8.4 %collective-permute-start.7 = (f32[528,128]{1,0:T(8,128)S(1)}, f32[528,128]{1,0:T(8,128)S(1)}, u32[]{:S(2)}, u32[]{:S(2)}) collective-permute-start(f32[528,128]{1,0:T(8,128)S(1)} %shard_map.72.refs_6_), channel_id=1, source_target_pairs={{1,3},{7,5},{8,10},{14,12},{17,19},{23,21},{24,26},{30,28}} | collective-permute-start | bytes 811016 | tf_op jit(solution)/shard_map/ppermute | solution.py:516
  26.5 10.0 %collective-permute-start.8 = (f32[528,128]{1,0:T(8,128)S(1)}, f32[528,128]{1,0:T(8,128)S(1)}, u32[]{:S(2)}, u32[]{:S(2)}) collective-permute-start(f32[528,128]{1,0:T(8,128)S(1)} %shard_map.73.refs_7_), channel_id=1, source_target_pairs={{1,3},{7,5},{8,10},{14,12},{17,19},{23,21},{24,26},{30,28}} | collective-permute-start | bytes 811016 | tf_op jit(solution)/shard_map/ppermute | solution.py:516
  38.0 1.4 %collective-permute-start.10 = (f32[1056,128]{1,0:T(8,128)S(1)}, f32[1056,128]{1,0:T(8,128)S(1)}, u32[]{:S(2)}, u32[]{:S(2)}) collective-permute-start(f32[1056,128]{1,0:T(8,128)S(1)} %get-tuple-element.60), channel_id=1, source_target_pairs={{3,5},{5,3},{10,12},{12,10},{19,21},{21,19},{26,28},{28,26}} | collective-permute-start | bytes 1622024 | tf_op jit(solution)/shard_map/ppermute | solution.py:516
  38.7 2.2 %collective-permute-start.9 = (f32[1056,128]{1,0:T(8,128)S(1)}, f32[1056,128]{1,0:T(8,128)S(1)}, u32[]{:S(2)}, u32[]{:S(2)}) collective-permute-start(f32[1056,128]{1,0:T(8,128)S(1)} %get-tuple-element.54), channel_id=1, source_target_pairs={{3,5},{5,3},{10,12},{12,10},{19,21},{21,19},{26,28},{28,26}} | collective-permute-start | bytes 1622024 | tf_op jit(solution)/shard_map/ppermute | solution.py:516
  40.0 3.5 %copy-start.1 = (f32[64,512]{1,0:T(8,128)S(1)}, f32[64,512]{1,0:T(8,128)}, u32[]{:S(2)}) copy-start(f32[64,512]{1,0:T(8,128)} %refs_0_.6) | copy-start | bytes 393220
  40.0 4.7 %collective-permute-start.14 = (f32[528,128]{1,0:T(8,128)S(1)}, f32[528,128]{1,0:T(8,128)S(1)}, u32[]{:S(2)}, u32[]{:S(2)}) collective-permute-start(f32[528,128]{1,0:T(8,128)S(1)} %get-tuple-element.62.refs_3_), channel_id=1, source_target_pairs={{3,2},{5,4},{10,11},{12,13},{19,18},{21,20},{26,27},{28,29}} | collective-permute-start | bytes 811016 | tf_op jit(solution)/shard_map/ppermute | solution.py:516
  41.4 3.3 %collective-permute-start.11 = (f32[528,128]{1,0:T(8,128)S(1)}, f32[528,128]{1,0:T(8,128)S(1)}, u32[]{:S(2)}, u32[]{:S(2)}) collective-permute-start(f32[528,128]{1,0:T(8,128)S(1)} %get-tuple-element.58.refs_0_), channel_id=1, source_target_pairs={{3,2},{5,4},{10,11},{12,13},{19,18},{21,20},{26,27},{28,29}} | collective-permute-start | bytes 811016 | tf_op jit(solution)/shard_map/ppermute | solution.py:516
  42.1 2.6 %collective-permute-start.12 = (f32[528,128]{1,0:T(8,128)S(1)}, f32[528,128]{1,0:T(8,128)S(1)}, u32[]{:S(2)}, u32[]{:S(2)}) collective-permute-start(f32[528,128]{1,0:T(8,128)S(1)} %get-tuple-element.59.refs_1_), channel_id=1, source_target_pairs={{3,2},{5,4},{10,11},{12,13},{19,18},{21,20},{26,27},{28,29}} | collective-permute-start | bytes 811016 | tf_op jit(solution)/shard_map/ppermute | solution.py:516
  42.8 2.0 %collective-permute-start.13 = (f32[528,128]{1,0:T(8,128)S(1)}, f32[528,128]{1,0:T(8,128)S(1)}, u32[]{:S(2)}, u32[]{:S(2)}) collective-permute-start(f32[528,128]{1,0:T(8,128)S(1)} %get-tuple-element.61.refs_2_), channel_id=1, source_target_pairs={{3,2},{5,4},{10,11},{12,13},{19,18},{21,20},{26,27},{28,29}} | collective-permute-start | bytes 811016 | tf_op jit(solution)/shard_map/ppermute | solution.py:516
  43.5 1.6 %collective-permute-start.4 = (f32[64,512]{1,0:T(8,128)S(1)}, f32[64,512]{1,0:T(8,128)S(1)}, u32[]{:S(2)}, u32[]{:S(2)}) collective-permute-start(f32[64,512]{1,0:T(8,128)S(1)} %copy-done.1), channel_id=1, source_target_pairs={{0,2},{1,3},{6,4},{7,5}} | collective-permute-start | bytes 393224 | tf_op jit(solution)/shard_map/ppermute | solution.py:516
  44.8 0.7 copy-start.2
  45.9 0.7 collective-permute-start.16
  47.0 0.7 collective-permute-start.17
  48.1 0.7 collective-permute-start.18
  48.8 44.6 %collective-permute-start.22 = (f32[64,512]{1,0:T(8,128)S(1)}, f32[64,512]{1,0:T(8,128)S(1)}, u32[]{:S(2)}, u32[]{:S(2)}) collective-permute-start(f32[64,512]{1,0:T(8,128)S(1)} %get-tuple-element.89), channel_id=1, source_target_pairs={{2,0},{3,1},{4,6},{5,7},{10,8},{11,9},{12,14},{13,15},{18,16},{19,... | collective-permute-start | bytes 393224 | tf_op jit(solution)/shard_map/ppermute | solution.py:516
  50.1 42.0 %copy-start = (bf16[2,512,512]{2,1,0:T(8,128)(2,1)S(1)}, bf16[2,512,512]{2,1,0:T(8,128)(2,1)}, u32[]{:S(2)}) copy-start(bf16[2,512,512]{2,1,0:T(8,128)(2,1)} %refs_7_.1) | copy-start | bytes 3145732
  50.4 2.8 %collective-permute-start.21 = (f32[8,512]{1,0:T(8,128)S(1)}, f32[8,512]{1,0:T(8,128)S(1)}, u32[]{:S(2)}, u32[]{:S(2)}) collective-permute-start(f32[8,512]{1,0:T(8,128)S(1)} %get-tuple-element.81.refs_0_), channel_id=1, source_target_pairs={{3,2},{5,4},{10,11},{12,13},{19,18},{21,20},{26,27},{28,29}} | collective-permute-start | bytes 49160 | tf_op jit(solution)/shard_map/ppermute | solution.py:516
  51.2 2.0 %collective-permute-start.20 = (f32[8,512]{1,0:T(8,128)S(1)}, f32[8,512]{1,0:T(8,128)S(1)}, u32[]{:S(2)}, u32[]{:S(2)}) collective-permute-start(f32[8,512]{1,0:T(8,128)S(1)} %get-tuple-element.82), channel_id=1, source_target_pairs={{3,0},{5,6},{10,9},{12,15},{19,16},{21,22},{26,25},{28,31}} | collective-permute-start | bytes 49160 | tf_op jit(solution)/shard_map/ppermute | solution.py:516
  51.9 40.2 %collective-permute-start.19 = (f32[8,512]{1,0:T(8,128)S(1)}, f32[8,512]{1,0:T(8,128)S(1)}, u32[]{:S(2)}, u32[]{:S(2)}) collective-permute-start(f32[8,512]{1,0:T(8,128)S(1)} %get-tuple-element.82), channel_id=1, source_target_pairs={{3,1},{5,7},{10,8},{12,14},{19,17},{21,23},{26,24},{28,30}} | collective-permute-start | bytes 49160 | tf_op jit(solution)/shard_map/ppermute | solution.py:516
